TPU v7x, 128 devices: a whole 4x4x4 slice. The times are simulated.
128 devices in a mesh: req: 16 (over x, z), exp: 8 (over y, core).
Axes of the slice: x: 4, y: 4, z: 4, core: 2. Of those that a mesh axis runs over, the one named last changes fastest.
Arguments:
- tokens: bfloat16 [16384, 2048], P('req'), may hold values from -40 to 40
- routes: int32 [16384, 2], P('req'), may hold values from 0 to 7, all different within a row; in each aligned block of 1024 rows (0 to 1023, 1024 to 2047, ...) at most 320 rows name the same one
- lengths: int32 [64], P('req'), may hold values from 1 to 256, 8192 in all
- cached_prefix_length: int32 [64], P('req'), may hold values from 0 to 64, as said below
- prefix_cache_row: int32 [64], replicated, may hold values from 0 to 15, as said below
- adapter_per_request: int32 [64], P('req'), may hold values from 0 to 63
- adapter_storage_slot: int32 [64], replicated, may hold values from 0 to 63, each once
- router_weight: bfloat16 [2048, 8], replicated, may hold values from -0.125 to 0.125
- key_value_weight: bfloat16 [2048, 4096], P('req', 'exp'), may hold values from -0.125 to 0.125
- expert_query_weight: bfloat16 [2048, 8, 2048], P('req', None, 'exp'), may hold values from -0.125 to 0.125
- expert_output_weight: bfloat16 [8, 2048, 2048], P(None, 'exp', 'req'), may hold values from -0.125 to 0.125
- adapter_down_maps: bfloat16 [64, 2048, 16], P('req'), may hold values from -0.125 to 0.125
- adapter_up_maps: bfloat16 [64, 16, 4096], P('req', None, 'exp'), may hold values from -1.5 to 1.5
- prefix_cache_store: bfloat16 [64, 64, 4096], P('req', None, 'exp'), may hold values from -6 to 6
Outputs:
- attention_out: bfloat16 [16384, 2048], P('req', 'exp')
Inputs may be any that keep to these rules, and one draw needn't show every extreme that they name: `routes`: in each aligned block of 1024 rows (one group) no expert is named by more than 320 rows, and one is named by exactly 320. The lengths sum to 8192 and some request has exactly 256. `cached_prefix_length`: exactly 32 requests have no cached prefix; some request has exactly 64. `prefix_cache_row`: request j of a group keeps its cache in slot j of its row; each row holds exactly one cache in each slot, and no row holds two caches of one group. `adapter_storage_slot`: each slot holds one adapter.
All inputs are finite; a program needn't handle non-finite values. No bound on the sum of `lengths` on one device may be relied on, other than what follows from the above.
Results may differ from a plain program's by a relative error of at most 0.017.
The roundings to bfloat16 on the way count: a program that leaves them out, or rounds other values in their place, can miss the bound.
Values may be sent and summed in bfloat16 or wider, within the bound.
No kernel may reach another device: no remote copies, remote signals or barrier semaphores. Data moves between devices by JAX's collectives and lax.ppermute only.
A program may use at most 128 MiB of HBM per device.

v0:
```python
import jax
import jax.numpy as jnp
from jax import lax
from jax.sharding import PartitionSpec as P

HD = 128
NE = 8
TOPK = 2
CAP = 320
adapter_scale = 0.5


def compact(routes):
    route_flat = routes.reshape(-1)
    pair_count = route_flat.shape[0]
    one_hot = (route_flat[:, None] == jnp.arange(NE, dtype=jnp.int32)[None, :]).astype(jnp.int32)
    earlier = jnp.cumsum(one_hot, axis=0) - one_hot
    route_rank = jnp.sum(earlier * one_hot, axis=1)
    slot_table = (
        jnp.zeros((NE, CAP), jnp.int32)
        .at[route_flat, route_rank]
        .set(jnp.arange(pair_count, dtype=jnp.int32))
    )
    return (route_flat, route_rank, slot_table)


def attend(queries, all_keys, cached_prefix_length):
    per_request = queries.shape[1]
    key_span = all_keys.shape[1]
    cached = key_span - per_request
    scores = jnp.einsum(
        "rtjhd,rshd->rhtjs", queries, all_keys[:, :, :, 0, :], preferred_element_type=jnp.float32
    ) * queries.shape[-1] ** (-0.5)
    key_place = jnp.arange(key_span, dtype=jnp.int32)
    query_place = jnp.arange(per_request, dtype=jnp.int32)
    from_cache = key_place[None, :] < cached_prefix_length[:, None]
    from_prompt = (key_place[None, :] >= cached) & (
        key_place[None, :] - cached <= query_place[:, None]
    )
    allowed = jnp.where(
        key_place[None, None, :] < cached, from_cache[:, None, :], from_prompt[None, :, :]
    )
    allowed = allowed[:, None, :, None, :]
    row_max = jnp.max(jnp.where(allowed, scores, -jnp.inf), axis=-1, keepdims=True)
    weights = jnp.where(allowed, jnp.exp(scores - row_max), 0.0)
    probability = (weights / jnp.sum(weights, axis=-1, keepdims=True)).astype(jnp.bfloat16)
    return jnp.einsum(
        "rhtjs,rshd->rtjhd",
        probability,
        all_keys[:, :, :, 1, :],
        preferred_element_type=jnp.float32,
    ).astype(jnp.bfloat16)


def body(
    tokens,
    routes,
    lengths,
    cached_prefix_length,
    prefix_cache_row,
    adapter_per_request,
    adapter_storage_slot,
    router_weight,
    key_value_weight,
    expert_query_weight,
    expert_output_weight,
    adapter_down_maps,
    adapter_up_maps,
    prefix_cache_store,
):
    group_index = lax.axis_index("req")
    num_requests = lengths.shape[0]
    tok_rows = tokens.shape[0]
    per_request = tok_rows // num_requests
    model_width = tokens.shape[1]
    kv_cols = key_value_weight.shape[1]
    query_cols = expert_query_weight.shape[2]
    heads = kv_cols // (2 * HD)
    cached = prefix_cache_store.shape[1]
    route_flat, route_rank, slot_table = compact(routes)
    picked = tokens[slot_table // 2]
    pieces = (
        lax.all_gather(key_value_weight, "req", axis=0, tiled=True),
        lax.all_gather(expert_query_weight, "req", axis=0, tiled=True),
    )
    key_value_segment = jnp.dot(tokens, pieces[0], preferred_element_type=jnp.float32)
    query_run = jnp.einsum("kcd,dkh->kch", picked, pieces[1], preferred_element_type=jnp.float32)
    adapter_hot = (
        adapter_per_request[:, None]
        == jnp.arange(adapter_storage_slot.shape[0], dtype=jnp.int32)[None, :]
    ).astype(jnp.int32)
    wanted = jnp.sum(adapter_hot * adapter_storage_slot[None, :], axis=1)
    pieces = (
        lax.all_gather(adapter_down_maps, "req", axis=0, tiled=True),
        lax.all_gather(adapter_up_maps, "req", axis=0, tiled=True),
    )
    row_count = pieces[0].shape[0]
    matches = (wanted[:, None] == jnp.arange(row_count, dtype=jnp.int32)[None, :]).astype(
        jnp.bfloat16
    )
    down_run = jnp.einsum("rn,ndq->rdq", matches, pieces[0], preferred_element_type=jnp.float32)
    up_run = jnp.einsum("rn,nqc->rqc", matches, pieces[1], preferred_element_type=jnp.float32)
    reduced_rank_state = jnp.einsum(
        "rtd,rdq->rtq",
        tokens.reshape(num_requests, per_request, model_width),
        down_run.astype(jnp.bfloat16),
        preferred_element_type=jnp.float32,
    ).astype(jnp.bfloat16)
    adapter_term = jnp.einsum(
        "mdg,mgy->mdy",
        reduced_rank_state,
        up_run.astype(jnp.bfloat16),
        preferred_element_type=jnp.float32,
    ).reshape(tok_rows, kv_cols)
    fresh_key_value = (key_value_segment + adapter_scale * adapter_term).astype(jnp.bfloat16)
    own_rows = lax.dynamic_slice_in_dim(
        prefix_cache_row, group_index * num_requests, num_requests, 0
    )
    wanted_slot = own_rows * num_requests + jnp.arange(num_requests, dtype=jnp.int32)
    shard_piece = lax.all_gather(prefix_cache_store, "req", axis=0, tiled=True)
    row_count = shard_piece.shape[0]
    matches = (wanted_slot[:, None] == jnp.arange(row_count, dtype=jnp.int32)[None, :]).astype(
        jnp.bfloat16
    )
    stored = jnp.einsum(
        "rn,nsc->rsc", matches, shard_piece, preferred_element_type=jnp.float32
    ).astype(jnp.bfloat16)
    all_keys = jnp.concatenate(
        [stored, fresh_key_value.reshape(num_requests, per_request, kv_cols)], axis=1
    )
    all_keys = all_keys.reshape(num_requests, cached + per_request, heads, 2, HD)
    queries = query_run.astype(jnp.bfloat16)[route_flat, route_rank].reshape(
        num_requests, per_request, TOPK, heads, HD
    )
    attended = attend(queries, all_keys, cached_prefix_length)
    gathered = attended.reshape(TOPK * tok_rows, query_cols)[slot_table]
    logits = jnp.dot(tokens, router_weight, preferred_element_type=jnp.float32)
    route_hot = (routes[:, :, None] == jnp.arange(NE, dtype=jnp.int32)[None, None, :]).astype(
        jnp.float32
    )
    chosen = jnp.sum(route_hot * logits[:, None, :], axis=-1)
    gate_values = jax.nn.sigmoid(chosen - chosen[:, ::-1])
    live_rows = (
        (jnp.arange(per_request, dtype=jnp.int32)[None, :] < lengths[:, None])
        .reshape(tok_rows)
        .astype(jnp.float32)
    )
    shard_piece = lax.all_gather(expert_output_weight, "req", axis=2, tiled=True)
    out_blocks = jnp.einsum(
        "kch,khn->kcn", gathered, shard_piece, preferred_element_type=jnp.float32
    )
    per_pair = out_blocks[route_flat, route_rank].reshape(tok_rows, TOPK, shard_piece.shape[2])
    partial_value = jnp.sum(per_pair * gate_values[:, :, None], axis=1) * live_rows[:, None]
    return lax.psum_scatter(
        partial_value.astype(jnp.bfloat16), "exp", scatter_dimension=1, tiled=True
    )


def solution(mesh):
    return jax.shard_map(
        body,
        mesh=mesh,
        in_specs=(
            P("req", None),
            P("req", None),
            P("req"),
            P("req"),
            P(),
            P("req"),
            P(),
            P(),
            P("req", "exp"),
            P("req", None, "exp"),
            P(None, "exp", "req"),
            P("req", None, None),
            P("req", None, "exp"),
            P("req", None, "exp"),
        ),
        out_specs=P("req", "exp"),
        check_vma=False,
    )
```

profile of v0, /device:TPU:0, one launch (start us, length us, event | category | flops | bytes accessed | tf_op | source)
XLA Modules:
  0.0 522.8 jit_solution(609906091671764247)
XLA Ops:
  6.5 0.7 all-gather.13.cloned.1.call-update
  7.3 0.7 all-gather.7.cloned.1.call-update
  8.1 0.7 all-gather.11.cloned.1.call-update
  8.8 0.5 all-gather.9.cloned.1.call-update
  9.4 1.9 copy.58
  11.4 0.5 all-gather.17.cloned.1.call-update
  12.0 0.9 copy.55
  12.9 0.3 eq.90
  13.2 0.3 eq.86
  13.4 0.3 reshape.176
  13.8 2.3 reduce-window.6
  16.0 0.3 slice_reduce_fusion
  16.3 0.2 reduce-window.9
  16.9 8.1 %scatter_custom_fusion = s32[2560]{0:T(1024)S(1)} fusion(s32[2048]{0:T(1024)S(1)} %broadcast_select_fusion.1, s32[2048]{0:T(1024)S(1)} %iota.56, s32[]{:T(128)} %constant.20.clone.1), kind=kCustom, calls=%fused_computation.75 | custom fusion | bytes 10244
  25.3 22.9 %gather_fusion = bf16[2560,2048]{1,0:T(8,128)(2,1)} fusion(bf16[1024,2048]{1,0:T(8,128)(2,1)} %param.14, s32[3072]{0:T(1024)S(1)} %pad_clamp_fusion.1), kind=kCustom, calls=%fused_computation | custom fusion | bytes 20981760 | tf_op jit(solution)/shard_map/gather | solution.py:81
  48.2 3.4 fusion.60
  51.7 0.4 rev.3
  52.1 0.2 copy.61
  52.6 0.2 select_reduce_fusion.2
  52.8 0.2 fusion.32
  53.0 0.3 broadcast_select_fusion
  53.3 1.6 all-gather.13.cloned.1.call-done
  54.8 3.0 convolution_convert_fusion.1
  57.9 50.1 %all-gather.7.cloned.1.call-done = bf16[64,64,512]{2,1,0:T(8,128)(2,1)} async-done(((bf16[4,64,512]{2,1,0:T(8,128)(2,1)}), bf16[64,64,512]{2,1,0:T(8,128)(2,1)}) %all-gather.7.cloned.1.call-update) | async-done | bytes 4194320 | tf_op jit(solution)/shard_map/all_gather | solution.py:120
  107.9 6.7 %fusion.21 = bf16[4,64,512]{2,0,1:T(4,128)(2,1)S(1)} fusion(bf16[64,64,512]{2,1,0:T(8,128)(2,1)} %all-gather.7.cloned.1.call-done, s32[4]{0:T(128)S(1)} %iota_add_fusion.1), kind=kOutput, calls=%fused_computation.29 | convolution fusion | flops 16908544 | bytes 4456464 | tf_op jit(solution)/shard_map/rn,nsc->rsc/dot_general | solution.py:125
  114.8 46.6 %all-gather.11.cloned.1.call-done = bf16[64,2048,16]{1,2,0:T(8,128)(2,1)} async-done(((bf16[4,2048,16]{1,2,0:T(8,128)(2,1)}), bf16[64,2048,16]{1,2,0:T(8,128)(2,1)}) %all-gather.11.cloned.1.call-update) | async-done | bytes 4194320 | tf_op jit(solution)/shard_map/all_gather | solution.py:94
  161.4 6.7 %fusion.15 = bf16[4,2048,16]{1,0,2:T(4,128)(2,1)S(1)} fusion(bf16[64,2048,16]{1,2,0:T(8,128)(2,1)} %all-gather.11.cloned.1.call-done, s32[4]{0:T(128)S(1)} %select_reduce_fusion.2), kind=kOutput, calls=%fused_computation.22 | convolution fusion | flops 16908544 | bytes 4456464 | tf_op jit(solution)/shard_map/rn,ndq->rdq/dot_general | solution.py:101
  168.1 4.0 convolution_multiply_fusion
  172.0 36.2 %all-gather.9.cloned.1.call-done = bf16[2048,512]{1,0:T(8,128)(2,1)} async-done(((bf16[128,512]{1,0:T(8,128)(2,1)}), bf16[2048,512]{1,0:T(8,128)(2,1)}) %all-gather.9.cloned.1.call-update) | async-done | bytes 2097168 | tf_op jit(solution)/shard_map/all_gather | solution.py:83
  208.2 6.2 %fusion.18 = bf16[1024,512]{1,0:T(8,128)(2,1)} fusion(f32[4,256,512]{2,1,0:T(8,128)S(1)} %convolution_multiply_fusion, bf16[1024,2048]{1,0:T(8,128)(2,1)} %param.14, bf16[2048,512]{1,0:T(8,128)(2,1)} %all-gather.9.cloned.1.call-done), kind=kOutput, calls=%fused_computation.24 | convolution fusion | flops 2148532224 | bytes 9437184 | tf_op jit(solution)/shard_map/dot_general | solution.py:86
  214.5 1.3 concatenate.14
  215.9 0.3 copy_dynamic-update-slice_fusion
  216.2 64.2 %all-gather.15.cloned.1.call-done = bf16[2048,8,256]{2,0,1:T(8,128)(2,1)} async-done(((bf16[128,8,256]{2,0,1:T(8,128)(2,1)}), bf16[2048,8,256]{2,0,1:T(8,128)(2,1)}) %all-gather.15.cloned.1.call-update) | async-done | bytes 8388624 | tf_op jit(solution)/shard_map/all_gather | solution.py:84
  280.4 9.2 %convolution_convert_fusion = bf16[8,320,256]{2,1,0:T(8,128)(2,1)S(1)} fusion(bf16[8,320,2048]{2,1,0:T(8,128)(2,1)} %bitcast.79, bf16[2048,8,256]{2,0,1:T(8,128)(2,1)} %all-gather.15.cloned.1.call-done), kind=kOutput, calls=%fused_computation.26 | convolution fusion | flops 2685009920 | bytes 20185088 | tf_op jit(solution)/shard_map/kcd,dkh->kch/dot_general | solution.py:87
  289.7 11.1 %gather_fusion.1 = bf16[2048,256]{1,0:T(8,128)(2,1)S(1)} fusion(bf16[8,320,256]{2,1,0:T(8,128)(2,1)S(1)} %convolution_convert_fusion, s32[2048]{0:T(1024)S(1)} %bitcast.76), kind=kCustom, calls=%fused_computation.1 | custom fusion | bytes 2113536 | tf_op jit(solution)/shard_map/gather | solution.py:132
  300.8 0.3 reshape.178
  301.1 6.3 %fusion.54 = (f32[4,2,256,2]{2,3,1,0:T(2,128)S(1)}, f32[4,2,256,2,320]{2,4,3,1,0:T(8,128)}) fusion(pred[4,256,320]{1,2,0:T(8,128)(4,1)S(1)} %broadcast_select_fusion, bf16[4,256,2,2,128]{4,3,2,1,0:T(2,128)(2,1)S(1)} %reshape.178, bf16[4,320,2,2,128]{4,1,2,0,3:T(8,128)(2,1)} %copy-done.2), kind=kOutput, calls=%fused_computation.96 | convolution fusion | flops 678953280 | bytes 9322496 | tf_op jit(solution)/shard_map/sub | solution.py:45
  307.4 3.3 fusion.20
  310.6 0.8 copy.60
  311.4 0.1 copy.98
  311.6 7.6 %gather_fusion.2 = bf16[2560,256]{1,0:T(8,128)(2,1)S(1)} fusion(bf16[2048,256]{1,0:T(8,128)(2,1)S(1)} %bitcast.78, s32[3072]{0:T(1024)S(1)} %pad_clamp_fusion), kind=kCustom, calls=%fused_computation.2 | custom fusion | bytes 2631680 | tf_op jit(solution)/shard_map/gather | solution.py:136
  319.2 41.3 %all-gather.17.cloned.1.call-done = bf16[8,256,2048]{2,1,0:T(8,128)(2,1)} async-done(((bf16[8,256,128]{2,1,0:T(8,128)(2,1)}), bf16[8,256,2048]{2,1,0:T(8,128)(2,1)}) %all-gather.17.cloned.1.call-update) | async-done | bytes 8388624 | tf_op jit(solution)/shard_map/all_gather | solution.py:148
  360.5 12.0 %fusion.59 = f32[8,320,2048]{2,1,0:T(8,128)} fusion(bf16[8,320,256]{2,1,0:T(8,128)(2,1)S(1)} %bitcast.80, bf16[8,256,2048]{2,1,0:T(8,128)(2,1)} %all-gather.17.cloned.1.call-done), kind=kOutput, calls=%fused_computation.97 | convolution fusion | flops 2684354560 | bytes 30670848 | tf_op jit(solution)/shard_map/kch,khn->kcn/dot_general | solution.py:149
  372.5 51.1 %gather_fusion.3 = f32[2048,2048]{1,0:T(8,128)} fusion(f32[8,320,2048]{2,1,0:T(8,128)} %fusion.59, s32[2048]{0:T(1024)S(1)} %bitcast.77), kind=kCustom, calls=%fused_computation.3 | custom fusion | bytes 33570816 | tf_op jit(solution)/shard_map/gather | solution.py:152
  423.6 20.0 %reshape.180 = f32[1024,2,2048]{2,1,0:T(2,128)} reshape(f32[2048,2048]{1,0:T(8,128)} %gather_fusion.3) | data formatting | bytes 33554432 | tf_op jit(solution)/shard_map/reshape | solution.py:152
  443.6 29.1 %multiply_reduce_fusion = f32[1024,2048]{1,0:T(8,128)} fusion(f32[1024,2,2048]{2,1,0:T(2,128)} %reshape.180, f32[1024,2]{1,0:T(8,128)S(1)} %copy.61), kind=kLoop, calls=%fused_computation.6 | loop fusion | flops 6291456 | bytes 25174016 | tf_op jit(solution)/shard_map/reduce_sum | solution.py:153
  472.8 5.8 %multiply_convert_fusion = bf16[1024,2048]{1,0:T(8,128)(2,1)} fusion(f32[1024,2048]{1,0:T(8,128)} %multiply_reduce_fusion, f32[1024]{0:T(1024)S(1)} %bitcast.83), kind=kLoop, calls=%fused_computation.7 | loop fusion | flops 4194304 | bytes 12587008 | tf_op jit(solution)/shard_map/convert_element_type | solution.py:155
  478.6 37.3 %reduce-scatter.2.cloned.1.call-done = bf16[1024,256]{1,0:T(8,128)(2,1)} async-done(((bf16[1024,2048]{1,0:T(8,128)(2,1)}), bf16[1024,256]{1,0:T(8,128)(2,1)}) %reduce-scatter.2.cloned.1.call-update) | async-done | bytes 524304 | tf_op jit(solution)/shard_map/reduce_scatter | solution.py:154
  (58 shorter events, 1.4 us)
Async XLA Ops:
  6.5 41.6 %copy-start = (bf16[2048,8]{0,1:T(8,128)(2,1)S(1)}, bf16[2048,8]{0,1:T(8,128)(2,1)}, u32[]{:S(2)}) copy-start(bf16[2048,8]{0,1:T(8,128)(2,1)} %param.21) | copy-start | bytes 98308
  6.5 10.2 %copy-start.7 = (s32[2]{0:T(128)S(1)}, s32[2]{0:T(128)}, u32[]{:S(2)}) copy-start(s32[2]{0:T(128)} %constant.62) | copy-start | bytes 28
  6.5 10.3 %copy-start.6 = (s32[2]{0:T(128)S(1)}, s32[2]{0:T(128)}, u32[]{:S(2)}) copy-start(s32[2]{0:T(128)} %constant.65) | copy-start | bytes 28
  6.5 48.3 %all-gather.13.cloned.1.call-start = ((), (), s32[]{:S(2)}) async-start(), calls=%async_computation.4 | async-start | bytes 1114112 | tf_op jit(solution)/shard_map/all_gather | solution.py:95
  7.3 100.7 %all-gather.7.cloned.1.call-start = ((), (), s32[]{:S(2)}) async-start(), calls=%async_computation.1 | async-start | bytes 4456448 | tf_op jit(solution)/shard_map/all_gather | solution.py:120
  8.0 153.3 %all-gather.11.cloned.1.call-start = ((), (), s32[]{:S(2)}) async-start(), calls=%async_computation.3 | async-start | bytes 4456448 | tf_op jit(solution)/shard_map/all_gather | solution.py:94
  8.7 199.5 %all-gather.9.cloned.1.call-start = ((), (), s32[]{:S(2)}) async-start(), calls=%async_computation.2 | async-start | bytes 2228224 | tf_op jit(solution)/shard_map/all_gather | solution.py:83
  9.3 271.1 %all-gather.15.cloned.1.call-start = ((), (), s32[]{:S(2)}) async-start(), calls=%async_computation.5 | async-start | bytes 8912896 | tf_op jit(solution)/shard_map/all_gather | solution.py:84
  11.3 349.2 %all-gather.17.cloned.1.call-start = ((), (), s32[]{:S(2)}) async-start(), calls=%async_computation.6 | async-start | bytes 8912896 | tf_op jit(solution)/shard_map/all_gather | solution.py:148
  11.9 504.0 %reduce-scatter.2.cloned.1.call-start = ((), (), s32[]{:S(2)}) async-start(), calls=%async_computation.7 | async-start | bytes 4718592 | tf_op jit(solution)/shard_map/reduce_scatter | solution.py:154
  48.1 3.5 copy-start.4
  48.1 4.2 copy-start.5
  48.1 4.3 copy-start.9
  48.2 4.4 copy-start.10
  48.2 4.4 copy-start.11
  48.2 4.6 copy-start.8
  216.2 64.2 %copy-start.2 = (bf16[4,320,2,2,128]{4,1,2,0,3:T(8,128)(2,1)}, bf16[4,320,2,2,128]{4,1,2,0,3:T(8,128)(2,1)S(1)}, u32[]{:S(2)}) copy-start(bf16[4,320,2,2,128]{4,1,2,0,3:T(8,128)(2,1)S(1)} %copy_dynamic-update-slice_fusion) | copy-start | bytes 3932164
  301.1 6.3 %copy-start.3 = (bf16[4,320,2,2,128]{4,1,2,0,3:T(8,128)(2,1)S(1)}, bf16[4,320,2,2,128]{4,1,2,0,3:T(8,128)(2,1)}, u32[]{:S(2)}) copy-start(bf16[4,320,2,2,128]{4,1,2,0,3:T(8,128)(2,1)} %copy-done.2) | copy-start | bytes 3932164
  472.8 43.2 %copy-start.1 = (bf16[2048,8]{0,1:T(8,128)(2,1)S(1)}, bf16[2048,8]{0,1:T(8,128)(2,1)}, u32[]{:S(2)}) copy-start(bf16[2048,8]{0,1:T(8,128)(2,1)} %param.21) | copy-start | bytes 98308
Sparse Core Ops, SparseCore 0:
  9.5 45.2 all-gather.12
  57.0 50.9 all-gather.6
  110.1 51.2 all-gather.10
  163.4 44.8 all-gather.8
  210.3 70.1 all-gather.14
  282.4 78.0 all-gather.16
  478.7 37.1 reduce-scatter.1
where the time goes:
time: 525 us; the launch traced here: 523 us
  waiting for transfers between devices  280 us (53%)
  local copies, waits for them, and re-layouts  129 us (25%)
  matrix products  60.9 us (12%)
  other arithmetic  38.7 us (7%)
  between operations  13.8 us (3%)
    all_gather x1, waiting for transfers between devices, body(): lax.all_gather(expert_query_weight, 'req', axis=0, tiled=True)  64.2 us
    gather x1, local copies, waits for them, and re-layouts, body(): out_blocks[route_flat, route_rank]  51.1 us
    all_gather x1, waiting for transfers between devices, body(): shard_piece = lax.all_gather(prefix_cache_store, 'req', axis=0, tiled=True)  50.1 us
    all_gather x1, waiting for transfers between devices, body(): lax.all_gather(adapter_down_maps, 'req', axis=0, tiled=True)  46.6 us
    all_gather x1, waiting for transfers between devices, body(): lax.all_gather(expert_output_weight, 'req', axis=2, tiled=True)  41.3 us
    reduce_scatter x1, waiting for transfers between devices, body(): lax.psum_scatter(partial_value.astype(jnp.bfloat16), 'exp', scatter_dimen...  37.3 us
    all_gather x1, waiting for transfers between devices, body(): lax.all_gather(key_value_weight, 'req', axis=0, tiled=True)  36.2 us
    reduce_sum x1, other arithmetic, body(): jnp.sum(per_pair * gate_values[:, :, None], axis=1) * live_rows[:, None]  29.1 us
  transfers between devices with their start and end apart: 7, of which 7 were waited for; matrix products, arithmetic and copies ran while one was open for 21% of the time, Pallas kernels for 0%

commit v1 on v0

--- a/solution.py
+++ b/solution.py
@@ -81,7 +81,10 @@
     picked = tokens[slot_table // 2]
     pieces = (
         lax.all_gather(key_value_weight, "req", axis=0, tiled=True),
-        lax.all_gather(expert_query_weight, "req", axis=0, tiled=True),
+        jnp.concatenate(
+            lax.all_to_all(jnp.stack([expert_query_weight] * lax.axis_size("req")), "req", 0, 0),
+            axis=0,
+        ),
     )
     key_value_segment = jnp.dot(tokens, pieces[0], preferred_element_type=jnp.float32)
     query_run = jnp.einsum("kcd,dkh->kch", picked, pieces[1], preferred_element_type=jnp.float32)

time: 525 us -> 559 us (1.065)
  local copies, waits for them, and re-layouts: 129 us -> 142 us
  waiting for transfers between devices: 280 us -> 290 us
  starting transfers between devices: 0.23 us -> 8.34 us
    all_gather x1, waiting for transfers between devices: 1.58 us -> 90.6 us  [body(): lax.all_gather(adapter_up_maps, 'req', axis=0, tiled=True)]
    all_gather x1 -> x0, waiting for transfers between devices: 64.2 us -> none  [body(): lax.all_gather(expert_query_weight, 'req', axis=0, tiled=True)]
    all_gather x1, waiting for transfers between devices: 50.1 us -> 11.3 us  [body(): shard_piece = lax.all_gather(prefix_cache_store, 'req', axis=0, tiled=True)]
    all_to_all x0 -> x1, waiting for transfers between devices: none -> 12.6 us  [body(): lax.all_to_all(jnp.stack([expert_query_weight] * lax.axis_size('req')), '...]
    all_gather x1, waiting for transfers between devices: 41.3 us -> 51.6 us  [body(): lax.all_gather(expert_output_weight, 'req', axis=2, tiled=True)]
    all_to_all x0 -> x1, starting transfers between devices: none -> 8.14 us  [body(): lax.all_to_all(jnp.stack([expert_query_weight] * lax.axis_size('req')), '...]
    all_to_all x0 -> x1, local copies, waits for them, and re-layouts: none -> 7.83 us  [body(): lax.all_to_all(jnp.stack([expert_query_weight] * lax.axis_size('req')), '...]
    unnamed x30 -> x28, local copies, waits for them, and re-layouts: 11.2 us -> 10.9 us
  transfers between devices with their start and end apart: 7 -> 7, of which waited for: 7 -> 7; matrix products, arithmetic and copies ran while one was open for 21% -> 22% of each run, Pallas kernels for 0% -> 0%
where the time goes in v1:
time: 559 us; the launch traced here: 554 us
  waiting for transfers between devices  290 us (52%)
  local copies, waits for them, and re-layouts  142 us (25%)
  matrix products  61.1 us (11%)
  other arithmetic  38.7 us (7%)
  between operations  14 us (3%)
  starting transfers between devices  8.34 us (1%)
    all_gather x1, waiting for transfers between devices, body(): lax.all_gather(adapter_up_maps, 'req', axis=0, tiled=True)  90.6 us
    all_gather x1, waiting for transfers between devices, body(): lax.all_gather(expert_output_weight, 'req', axis=2, tiled=True)  51.6 us
    gather x1, local copies, waits for them, and re-layouts, body(): out_blocks[route_flat, route_rank]  51.1 us
    all_gather x1, waiting for transfers between devices, body(): lax.all_gather(adapter_down_maps, 'req', axis=0, tiled=True)  46.6 us
    reduce_scatter x1, waiting for transfers between devices, body(): lax.psum_scatter(partial_value.astype(jnp.bfloat16), 'exp', scatter_dimen...  37.3 us
    all_gather x1, waiting for transfers between devices, body(): lax.all_gather(key_value_weight, 'req', axis=0, tiled=True)  36.4 us
    reduce_sum x1, other arithmetic, body(): jnp.sum(per_pair * gate_values[:, :, None], axis=1) * live_rows[:, None]  29.1 us
    gather x1, local copies, waits for them, and re-layouts, body(): picked = tokens[slot_table // 2]  22.9 us
  transfers between devices with their start and end apart: 7, of which 7 were waited for; matrix products, arithmetic and copies ran while one was open for 22% of the time, Pallas kernels for 0%

profile of v1, /device:TPU:0, one launch (start us, length us, event | category | flops | bytes accessed | tf_op | source)
XLA Modules:
  0.0 554.1 jit_solution(10585575856939187122)
XLA Ops:
  6.5 0.7 all-gather.12.cloned.1.call-update
  7.3 0.7 all-gather.6.cloned.1.call-update
  8.1 0.7 all-gather.10.cloned.1.call-update
  8.8 0.5 all-gather.8.cloned.1.call-update
  9.4 0.5 all-gather.14.cloned.1.call-update
  9.9 1.1 copy.59
  11.1 4.4 stack.2
  15.4 8.1 %all-to-all-start = ((bf16[16,128,8,256]{3,1,2,0:T(8,128)(2,1)}), bf16[16,128,8,256]{3,1,2,0:T(8,128)(2,1)}, u32[]{:S(2)}, u32[]{:S(2)}) async-start(bf16[16,128,8,256]{3,1,2,0:T(8,128)(2,1)} %stack.2), calls=%async_computation | async-start | bytes 16777216 | tf_op jit(solution)/shard_map/all_to_all | solution.py:85
  23.7 0.2 copy.56
  23.9 0.3 eq.90
  24.2 0.3 eq.86
  24.4 0.3 reshape.181
  24.8 2.3 reduce-window.6
  27.0 0.3 slice_reduce_fusion
  27.9 8.5 %scatter_custom_fusion = s32[2560]{0:T(1024)S(1)} fusion(s32[2048]{0:T(1024)S(1)} %broadcast_select_fusion.1, s32[2048]{0:T(1024)S(1)} %iota.56, s32[]{:T(128)} %constant.20.clone.1), kind=kCustom, calls=%fused_computation.75 | custom fusion | bytes 10244
  36.7 22.9 %gather_fusion = bf16[2560,2048]{1,0:T(8,128)(2,1)} fusion(bf16[1024,2048]{1,0:T(8,128)(2,1)} %param.14, s32[3072]{0:T(1024)S(1)} %pad_clamp_fusion.1), kind=kCustom, calls=%fused_computation | custom fusion | bytes 20981760 | tf_op jit(solution)/shard_map/gather | solution.py:81
  59.6 3.4 fusion.60
  63.1 0.2 rev.3
  63.4 0.2 copy.63
  64.2 0.3 broadcast_select_fusion
  64.5 90.6 %all-gather.12.cloned.1.call-done = bf16[64,16,512]{2,1,0:T(8,128)(2,1)} async-done(((bf16[4,16,512]{2,1,0:T(8,128)(2,1)}), bf16[64,16,512]{2,1,0:T(8,128)(2,1)}) %all-gather.12.cloned.1.call-update) | async-done | bytes 1048592 | tf_op jit(solution)/shard_map/all_gather | solution.py:98
  155.1 3.1 convolution_convert_fusion.1
  158.2 12.6 %all-to-all-done = bf16[16,128,8,256]{3,1,2,0:T(8,128)(2,1)} async-done(((bf16[16,128,8,256]{3,1,2,0:T(8,128)(2,1)}), bf16[16,128,8,256]{3,1,2,0:T(8,128)(2,1)}, u32[]{:S(2)}, u32[]{:S(2)}) %all-to-all-start) | async-done | bytes 8388640 | tf_op jit(solution)/shard_map/all_to_all | solution.py:85
  170.7 7.8 %copy.60 = bf16[16,128,8,256]{3,1,0,2:T(8,128)(2,1)} copy(bf16[16,128,8,256]{3,1,2,0:T(8,128)(2,1)} %all-to-all-done) | data formatting | bytes 16777216 | tf_op jit(solution)/shard_map/all_to_all | solution.py:85
  178.6 9.3 %convolution_convert_fusion = bf16[8,320,256]{2,1,0:T(8,128)(2,1)S(1)} fusion(bf16[8,320,2048]{2,1,0:T(8,128)(2,1)} %bitcast.80, bf16[2048,8,256]{2,0,1:T(8,128)(2,1)} %bitcast.81), kind=kOutput, calls=%fused_computation.26 | convolution fusion | flops 2685009920 | bytes 20185088 | tf_op jit(solution)/shard_map/kcd,dkh->kch/dot_general | solution.py:90
  187.8 11.1 %gather_fusion.1 = bf16[2048,256]{1,0:T(8,128)(2,1)S(1)} fusion(bf16[8,320,256]{2,1,0:T(8,128)(2,1)S(1)} %convolution_convert_fusion, s32[2048]{0:T(1024)S(1)} %bitcast.77), kind=kCustom, calls=%fused_computation.1 | custom fusion | bytes 2113536 | tf_op jit(solution)/shard_map/gather | solution.py:135
  199.0 1.3 reshape.184
  200.2 11.3 %all-gather.6.cloned.1.call-done = bf16[64,64,512]{2,1,0:T(8,128)(2,1)} async-done(((bf16[4,64,512]{2,1,0:T(8,128)(2,1)}), bf16[64,64,512]{2,1,0:T(8,128)(2,1)}) %all-gather.6.cloned.1.call-update) | async-done | bytes 4194320 | tf_op jit(solution)/shard_map/all_gather | solution.py:123
  211.6 6.7 %fusion.21 = bf16[4,64,512]{2,0,1:T(4,128)(2,1)S(1)} fusion(bf16[64,64,512]{2,1,0:T(8,128)(2,1)} %all-gather.6.cloned.1.call-done, s32[4]{0:T(128)S(1)} %iota_add_fusion.1), kind=kOutput, calls=%fused_computation.29 | convolution fusion | flops 16908544 | bytes 4456464 | tf_op jit(solution)/shard_map/rn,nsc->rsc/dot_general | solution.py:128
  218.4 46.6 %all-gather.10.cloned.1.call-done = bf16[64,2048,16]{1,2,0:T(8,128)(2,1)} async-done(((bf16[4,2048,16]{1,2,0:T(8,128)(2,1)}), bf16[64,2048,16]{1,2,0:T(8,128)(2,1)}) %all-gather.10.cloned.1.call-update) | async-done | bytes 4194320 | tf_op jit(solution)/shard_map/all_gather | solution.py:97
  265.0 6.7 %fusion.15 = bf16[4,2048,16]{1,0,2:T(4,128)(2,1)S(1)} fusion(bf16[64,2048,16]{1,2,0:T(8,128)(2,1)} %all-gather.10.cloned.1.call-done, s32[4]{0:T(128)S(1)} %select_reduce_fusion.2), kind=kOutput, calls=%fused_computation.22 | convolution fusion | flops 16908544 | bytes 4456464 | tf_op jit(solution)/shard_map/rn,ndq->rdq/dot_general | solution.py:104
  271.7 3.8 convolution_multiply_fusion
  275.5 36.4 %all-gather.8.cloned.1.call-done = bf16[2048,512]{1,0:T(8,128)(2,1)} async-done(((bf16[128,512]{1,0:T(8,128)(2,1)}), bf16[2048,512]{1,0:T(8,128)(2,1)}) %all-gather.8.cloned.1.call-update) | async-done | bytes 2097168 | tf_op jit(solution)/shard_map/all_gather | solution.py:83
  311.8 6.4 %fusion.18 = bf16[1024,512]{1,0:T(8,128)(2,1)} fusion(f32[4,256,512]{2,1,0:T(8,128)S(1)} %convolution_multiply_fusion, bf16[1024,2048]{1,0:T(8,128)(2,1)} %param.14, bf16[2048,512]{1,0:T(8,128)(2,1)} %all-gather.8.cloned.1.call-done), kind=kOutput, calls=%fused_computation.24 | convolution fusion | flops 2148532224 | bytes 9437184 | tf_op jit(solution)/shard_map/dot_general | solution.py:89
  318.3 1.4 concatenate.14
  319.7 0.8 copy_dynamic-update-slice_fusion.1
  320.5 1.2 copy_dynamic-update-slice_fusion
  321.7 6.3 %fusion.54 = (f32[4,2,256,2]{2,3,1,0:T(2,128)S(1)}, f32[4,2,256,2,320]{2,4,3,1,0:T(8,128)}) fusion(pred[4,256,320]{1,2,0:T(8,128)(4,1)S(1)} %broadcast_select_fusion, bf16[4,256,2,2,128]{4,3,2,1,0:T(2,128)(2,1)S(1)} %copy-done.2, bf16[4,320,2,2,128]{4,1,2,0,3:T(8,128)(2,1)} %copy_dynamic-update-slice_fusion), kind=kOutput, calls=%fused_computation.96 | convolution fusion | flops 678953280 | bytes 9322496 | tf_op jit(solution)/shard_map/sub | solution.py:45
  328.0 3.5 fusion.20
  331.5 0.8 copy.62
  332.4 7.6 %gather_fusion.2 = bf16[2560,256]{1,0:T(8,128)(2,1)S(1)} fusion(bf16[2048,256]{1,0:T(8,128)(2,1)S(1)} %bitcast.79, s32[3072]{0:T(1024)S(1)} %pad_clamp_fusion), kind=kCustom, calls=%fused_computation.2 | custom fusion | bytes 2631680 | tf_op jit(solution)/shard_map/gather | solution.py:139
  340.0 51.6 %all-gather.14.cloned.1.call-done = bf16[8,256,2048]{2,1,0:T(8,128)(2,1)} async-done(((bf16[8,256,128]{2,1,0:T(8,128)(2,1)}), bf16[8,256,2048]{2,1,0:T(8,128)(2,1)}) %all-gather.14.cloned.1.call-update) | async-done | bytes 8388624 | tf_op jit(solution)/shard_map/all_gather | solution.py:151
  391.6 12.0 %fusion.59 = f32[8,320,2048]{2,1,0:T(8,128)} fusion(bf16[8,320,256]{2,1,0:T(8,128)(2,1)S(1)} %bitcast.82, bf16[8,256,2048]{2,1,0:T(8,128)(2,1)} %all-gather.14.cloned.1.call-done), kind=kOutput, calls=%fused_computation.97 | convolution fusion | flops 2684354560 | bytes 30670848 | tf_op jit(solution)/shard_map/kch,khn->kcn/dot_general | solution.py:152
  403.6 51.1 %gather_fusion.3 = f32[2048,2048]{1,0:T(8,128)} fusion(f32[8,320,2048]{2,1,0:T(8,128)} %fusion.59, s32[2048]{0:T(1024)S(1)} %bitcast.78), kind=kCustom, calls=%fused_computation.3 | custom fusion | bytes 33570816 | tf_op jit(solution)/shard_map/gather | solution.py:155
  454.7 20.0 %reshape.186 = f32[1024,2,2048]{2,1,0:T(2,128)} reshape(f32[2048,2048]{1,0:T(8,128)} %gather_fusion.3) | data formatting | bytes 33554432 | tf_op jit(solution)/shard_map/reshape | solution.py:155
  474.7 29.1 %multiply_reduce_fusion = f32[1024,2048]{1,0:T(8,128)} fusion(f32[1024,2,2048]{2,1,0:T(2,128)} %reshape.186, f32[1024,2]{1,0:T(8,128)S(1)} %copy.63), kind=kLoop, calls=%fused_computation.6 | loop fusion | flops 6291456 | bytes 25174016 | tf_op jit(solution)/shard_map/reduce_sum | solution.py:156
  503.8 5.8 %multiply_convert_fusion = bf16[1024,2048]{1,0:T(8,128)(2,1)} fusion(f32[1024,2048]{1,0:T(8,128)} %multiply_reduce_fusion, f32[1024]{0:T(1024)S(1)} %bitcast.85), kind=kLoop, calls=%fused_computation.7 | loop fusion | flops 4194304 | bytes 12587008 | tf_op jit(solution)/shard_map/convert_element_type | solution.py:158
  509.7 37.3 %reduce-scatter.2.cloned.1.call-done = bf16[1024,256]{1,0:T(8,128)(2,1)} async-done(((bf16[1024,2048]{1,0:T(8,128)(2,1)}), bf16[1024,256]{1,0:T(8,128)(2,1)}) %reduce-scatter.2.cloned.1.call-update) | async-done | bytes 524304 | tf_op jit(solution)/shard_map/reduce_scatter | solution.py:157
  (57 shorter events, 2.0 us)
Async XLA Ops:
  6.5 53.1 %copy-start = (bf16[2048,8]{0,1:T(8,128)(2,1)S(1)}, bf16[2048,8]{0,1:T(8,128)(2,1)}, u32[]{:S(2)}) copy-start(bf16[2048,8]{0,1:T(8,128)(2,1)} %param.21) | copy-start | bytes 98308
  6.5 148.6 %all-gather.12.cloned.1.call-start = ((), (), s32[]{:S(2)}) async-start(), calls=%async_computation.5 | async-start | bytes 1114112 | tf_op jit(solution)/shard_map/all_gather | solution.py:98
  7.3 204.3 %all-gather.6.cloned.1.call-start = ((), (), s32[]{:S(2)}) async-start(), calls=%async_computation.2 | async-start | bytes 4456448 | tf_op jit(solution)/shard_map/all_gather | solution.py:123
  8.0 257.0 %all-gather.10.cloned.1.call-start = ((), (), s32[]{:S(2)}) async-start(), calls=%async_computation.4 | async-start | bytes 4456448 | tf_op jit(solution)/shard_map/all_gather | solution.py:97
  8.7 303.1 %all-gather.8.cloned.1.call-start = ((), (), s32[]{:S(2)}) async-start(), calls=%async_computation.3 | async-start | bytes 2228224 | tf_op jit(solution)/shard_map/all_gather | solution.py:83
  9.3 382.3 %all-gather.14.cloned.1.call-start = ((), (), s32[]{:S(2)}) async-start(), calls=%async_computation.6 | async-start | bytes 8912896 | tf_op jit(solution)/shard_map/all_gather | solution.py:151
  15.4 8.2 %copy-start.3 = (s32[1024,2]{0,1:T(2,128)S(1)}, s32[1024,2]{0,1:T(2,128)}, u32[]{:S(2)}) copy-start(s32[1024,2]{0,1:T(2,128)} %param.15) | copy-start | bytes 24580
  15.4 12.3 %copy-start.6 = (s32[2]{0:T(128)S(1)}, s32[2]{0:T(128)}, u32[]{:S(2)}) copy-start(s32[2]{0:T(128)} %constant.62) | copy-start | bytes 28
  15.4 12.4 %copy-start.5 = (s32[2]{0:T(128)S(1)}, s32[2]{0:T(128)}, u32[]{:S(2)}) copy-start(s32[2]{0:T(128)} %constant.65) | copy-start | bytes 28
  15.4 155.3 %all-to-all-start = ((bf16[16,128,8,256]{3,1,2,0:T(8,128)(2,1)}), bf16[16,128,8,256]{3,1,2,0:T(8,128)(2,1)}, u32[]{:S(2)}, u32[]{:S(2)}) async-start(bf16[16,128,8,256]{3,1,2,0:T(8,128)(2,1)} %stack.2), calls=%async_computation | async-start | bytes 16777216 | tf_op jit(solution)/shard_map/all_to_all | solution.py:85
  23.6 523.4 %reduce-scatter.2.cloned.1.call-start = ((), (), s32[]{:S(2)}) async-start(), calls=%async_computation.7 | async-start | bytes 4718592 | tf_op jit(solution)/shard_map/reduce_scatter | solution.py:157
  59.6 4.0 copy-start.4
  59.6 4.1 copy-start.8
  59.6 4.2 copy-start.9
  59.6 4.2 copy-start.10
  59.6 4.4 copy-start.7
  318.3 3.5 copy-start.2
  503.8 43.2 %copy-start.1 = (bf16[2048,8]{0,1:T(8,128)(2,1)S(1)}, bf16[2048,8]{0,1:T(8,128)(2,1)}, u32[]{:S(2)}) copy-start(bf16[2048,8]{0,1:T(8,128)(2,1)} %param.21) | copy-start | bytes 98308
Sparse Core Ops, SparseCore 0:
  9.5 145.5 all-gather.11
  157.2 54.2 all-gather.5
  213.7 51.2 all-gather.9
  267.0 44.8 all-gather.7
  313.8 77.7 all-gather.13
  509.8 37.1 reduce-scatter.1
